TPU v7x, 32 devices: a whole 2x2x4 slice. The times are simulated.
32 devices in a mesh: rows: 16 (over z, x, core), feat: 2 (over y).
Axes of the slice: x: 2, y: 2, z: 4, core: 2. Of those that a mesh axis runs over, the one named last changes fastest.
Arguments:
- gradients: bfloat16 [16384, 8192], P('rows', 'feat'), may hold values from -2500 to 2500
- queries: bfloat16 [1024, 8192], P('rows', 'feat'), may hold values from -0.09375 to 0.09375
- loss_weight: float32 [16384], P('rows'), may hold values from 0.09 to 1
Outputs:
- standardized: bfloat16 [16384, 1024], P('rows', 'feat')
All inputs are finite; a program needn't handle non-finite values.
Results may differ from a plain program's by a relative error of at most 0.019.
Values may be sent and summed in bfloat16 or wider, within the bound.
No kernel may reach another device: no remote copies, remote signals or barrier semaphores. Data moves between devices by JAX's collectives and lax.ppermute only.
A program may use at most 64 MiB of HBM per device.

v0:
```python
import jax
import jax.numpy as jnp
from jax import lax
from jax.sharding import PartitionSpec as P

NORM_EPS = 1e-06
VAR_EPS = 1e-05


def body(gradients, queries, loss_weight):
    rows_here = gradients.shape[0]
    total_rows = rows_here * lax.axis_size("rows")
    feature_count = gradients.shape[1] * lax.axis_size("feat")
    local_squares = jnp.sum(jnp.square(gradients.astype(jnp.float32)), axis=1)
    squares = lax.psum(local_squares, "feat")
    product = lax.dot_general(
        gradients,
        lax.all_gather(queries, "rows", axis=0, tiled=True),
        (((1,), (1,)), ((), ())),
        preferred_element_type=jnp.float32,
    )
    partial_value = product.astype(jnp.bfloat16)
    partial_float = partial_value.astype(jnp.float32)
    raw = lax.psum_scatter(
        partial_float.astype(jnp.bfloat16), "feat", scatter_dimension=1, tiled=True
    ).astype(jnp.float32)
    factor = loss_weight / jnp.sqrt(squares / feature_count + NORM_EPS)
    scored = raw * factor[:, None]
    sums = lax.psum(jnp.sum(scored, axis=0), "rows")
    column_mean = sums / total_rows
    centered = scored - column_mean[None, :]
    square_sums = lax.psum(jnp.sum(centered * centered, axis=0), "rows")
    column_var = square_sums / total_rows
    return (centered * lax.rsqrt(column_var + VAR_EPS)[None, :]).astype(jnp.bfloat16)


def solution(mesh):
    in_specs = (P("rows", "feat"), P("rows", "feat"), P("rows"))
    out_specs = P("rows", "feat")
    return jax.shard_map(body, mesh=mesh, in_specs=in_specs, out_specs=out_specs, check_vma=False)
```

profile of v0, /device:TPU:0, one launch (start us, length us, event | category | flops | bytes accessed | tf_op | source)
XLA Modules:
  0.0 206.0 jit_solution(2264550643028440767)
XLA Ops:
  6.5 0.0 all-gather.2.cloned.1.call-start
  6.5 0.7 all-gather.2.cloned.1.call-update
  7.3 0.0 reduce-scatter.2.cloned.1.call-start
  7.3 79.2 %all-gather.2.cloned.1.call-done = bf16[1024,4096]{1,0:T(8,128)(2,1)} async-done(((bf16[64,4096]{1,0:T(8,128)(2,1)}), bf16[1024,4096]{1,0:T(8,128)(2,1)}) %all-gather.2.cloned.1.call-update) | async-done | bytes 8388624 | tf_op jit(solution)/shard_map/all_gather | solution.py:18
  86.5 14.7 %convolution_convert_fusion = bf16[1024,1024]{1,0:T(8,128)(2,1)} fusion(bf16[1024,4096]{1,0:T(8,128)(2,1)} %param.3, bf16[1024,4096]{1,0:T(8,128)(2,1)} %all-gather.2.cloned.1.call-done), kind=kOutput, calls=%fused_computation.6 | convolution fusion | flops 8590983168 | bytes 18874368 | tf_op jit(solution)/shard_map/dot_general | solution.py:16
  101.3 0.0 reduce-scatter.2.cloned.1.call-update
  101.3 0.0 copy-start.1
  101.3 5.1 %multiply_reduce_fusion = f32[1024]{0:T(1024)S(1)} fusion(bf16[1024,4096]{1,0:T(8,128)(2,1)} %param.3), kind=kLoop, calls=%fused_computation | loop fusion | flops 12581888 | bytes 8392704 | tf_op jit(solution)/shard_map/reduce_sum | solution.py:14
  106.4 5.1 %psum.21 = f32[1024]{0:T(1024)S(1)} all-reduce(f32[1024]{0:T(1024)S(1)} %multiply_reduce_fusion), channel_id=1, replica_groups=mesh['rows'=16,'feat'=2] {'feat'}, use_global_device_ids=true, to_apply=%region_2.0 | all-reduce | flops 1024 | bytes 8192 | tf_op jit(solution)/shard_map/psum | solution.py:15
  111.5 0.0 copy-done.1
  111.6 20.5 %reduce-scatter.2.cloned.1.call-done = bf16[1024,512]{1,0:T(8,128)(2,1)} async-done(((bf16[1024,1024]{1,0:T(8,128)(2,1)}), bf16[1024,512]{1,0:T(8,128)(2,1)}) %reduce-scatter.2.cloned.1.call-update) | async-done | bytes 1048592 | tf_op jit(solution)/shard_map/reduce_scatter | solution.py:24
  132.1 0.0 copy-start
  132.1 1.6 fusion.1
  133.7 33.0 %psum.22 = f32[512]{0:T(512)S(1)} all-reduce(f32[512]{0:T(512)S(1)} %fusion.1), channel_id=1, replica_groups=mesh['rows'=16,'feat'=2] {'rows'}, use_global_device_ids=true, to_apply=%region_4.0 | all-reduce | flops 512 | bytes 4096 | tf_op jit(solution)/shard_map/psum | solution.py:29
  166.7 1.6 multiply_reduce_fusion.1
  168.3 29.5 %psum.23 = f32[512]{0:T(512)S(1)} all-reduce(f32[512]{0:T(512)S(1)} %multiply_reduce_fusion.1), channel_id=1, replica_groups=mesh['rows'=16,'feat'=2] {'rows'}, use_global_device_ids=true, to_apply=%region_6.0 | all-reduce | flops 512 | bytes 4096 | tf_op jit(solution)/shard_map/psum | solution.py:32
  197.8 0.0 copy-done
  197.8 1.3 multiply_convert_fusion
  (3 shorter events, 0.0 us)
Async XLA Ops:
  6.5 80.0 %all-gather.2.cloned.1.call-start = ((), (), s32[]{:S(2)}) async-start(), calls=%async_computation.1 | async-start | bytes 8912896 | tf_op jit(solution)/shard_map/all_gather | solution.py:18
  7.3 124.8 %reduce-scatter.2.cloned.1.call-start = ((), (), s32[]{:S(2)}) async-start(), calls=%async_computation.2 | async-start | bytes 3145728 | tf_op jit(solution)/shard_map/reduce_scatter | solution.py:24
  101.3 10.2 %copy-start.1 = (f32[1024]{0:T(1024)S(1)}, f32[1024]{0:T(1024)}, u32[]{:S(2)}) copy-start(f32[1024]{0:T(1024)} %param.5) | copy-start | bytes 12292
  132.1 65.8 %copy-start = (bf16[1024,512]{1,0:T(8,128)(2,1)S(1)}, bf16[1024,512]{1,0:T(8,128)(2,1)}, u32[]{:S(2)}) copy-start(bf16[1024,512]{1,0:T(8,128)(2,1)} %reduce-scatter.2.cloned.1.call-done) | copy-start | bytes 3145732
Sparse Core Ops, SparseCore 0:
  9.5 77.0 all-gather.1
  101.4 30.5 reduce-scatter.1
where the time goes:
time: 206 us
  waiting for transfers between devices  100 us (49%)
  blocking collectives  67.7 us (33%)
  matrix products  14.7 us (7%)
  between operations  13.4 us (7%)
  other arithmetic  9.68 us (5%)
    all_gather x1, waiting for transfers between devices, body(): lax.all_gather(queries, 'rows', axis=0, tiled=True)  79.2 us
    psum x1, blocking collectives, body(): sums = lax.psum(jnp.sum(scored, axis=0), 'rows')  33 us
    psum x1, blocking collectives, body(): square_sums = lax.psum(jnp.sum(centered * centered, axis=0), 'rows')  29.5 us
    reduce_scatter x1, waiting for transfers between devices, body(): lax.psum_scatter(partial_float.astype(jnp.bfloat16), 'feat', scatter_dime...  20.5 us
    dot_general x1, matrix products, body(): lax.dot_general(gradients, lax.all_gather(queries, 'rows', axis=0, tiled=...  14.7 us
    psum x1, blocking collectives, body(): squares = lax.psum(local_squares, 'feat')  5.15 us
    reduce_sum x1, other arithmetic, body(): local_squares = jnp.sum(jnp.square(gradients.astype(jnp.float32)), axis=1)  5.08 us
  transfers between devices with their start and end apart: 2, of which 2 were waited for; matrix products, arithmetic and copies ran while one was open for 2% of the time, Pallas kernels for 0%

commit v1 on v0

--- a/solution.py
+++ b/solution.py
@@ -1,10 +1,20 @@
+import functools
 import jax
 import jax.numpy as jnp
 from jax import lax
 from jax.sharding import PartitionSpec as P
+from jax.lax import all_gather
 
 NORM_EPS = 1e-06
 VAR_EPS = 1e-05
+
+
+def step_on_pieces_all(m, axis_tag):
+    x_next = all_gather(m, axis_name=axis_tag)
+    return jnp.sum(x_next, 0)
+
+
+_begin_space = functools.partial(step_on_pieces_all, axis_tag="rows")
 
 
 def body(gradients, queries, loss_weight):
@@ -29,7 +39,7 @@
     sums = lax.psum(jnp.sum(scored, axis=0), "rows")
     column_mean = sums / total_rows
     centered = scored - column_mean[None, :]
-    square_sums = lax.psum(jnp.sum(centered * centered, axis=0), "rows")
+    square_sums = _begin_space(jnp.sum(centered * centered, axis=0))
     column_var = square_sums / total_rows
     return (centered * lax.rsqrt(column_var + VAR_EPS)[None, :]).astype(jnp.bfloat16)
 

time: 206 us -> 194 us (0.942)
  blocking collectives: 67.7 us -> 55.4 us
    psum x1 -> x0, blocking collectives: 29.5 us -> none  [body(): square_sums = lax.psum(jnp.sum(centered * centered, axis=0), 'rows')]
    all_gather x0 -> x1, blocking collectives: none -> 17.2 us  [step_on_pieces_all(): x_next = all_gather(m, axis_name=axis_tag)]
  transfers between devices with their start and end apart: 2 -> 2, of which waited for: 2 -> 2; matrix products, arithmetic and copies ran while one was open for 2% -> 3% of each run, Pallas kernels for 0% -> 0%
where the time goes in v1:
time: 194 us
  waiting for transfers between devices  100 us (52%)
  blocking collectives  55.4 us (29%)
  matrix products  14.7 us (8%)
  between operations  13.4 us (7%)
  other arithmetic  9.72 us (5%)
    all_gather x1, waiting for transfers between devices, body(): lax.all_gather(queries, 'rows', axis=0, tiled=True)  79.2 us
    psum x1, blocking collectives, body(): sums = lax.psum(jnp.sum(scored, axis=0), 'rows')  33 us
    reduce_scatter x1, waiting for transfers between devices, body(): lax.psum_scatter(partial_float.astype(jnp.bfloat16), 'feat', scatter_dime...  20.5 us
    all_gather x1, blocking collectives, step_on_pieces_all(): x_next = all_gather(m, axis_name=axis_tag)  17.2 us
    dot_general x1, matrix products, body(): lax.dot_general(gradients, lax.all_gather(queries, 'rows', axis=0, tiled=...  14.7 us
    psum x1, blocking collectives, body(): squares = lax.psum(local_squares, 'feat')  5.15 us
    reduce_sum x1, other arithmetic, body(): local_squares = jnp.sum(jnp.square(gradients.astype(jnp.float32)), axis=1)  5.08 us
  transfers between devices with their start and end apart: 2, of which 2 were waited for; matrix products, arithmetic and copies ran while one was open for 3% of the time, Pallas kernels for 0%

profile of v1, /device:TPU:0, one launch (start us, length us, event | category | flops | bytes accessed | tf_op | source)
XLA Modules:
  0.0 193.8 jit_solution(1940195850533825410)
XLA Ops:
  6.5 0.0 all-gather.4.cloned.1.call-start
  6.5 0.7 all-gather.4.cloned.1.call-update
  7.3 0.0 reduce-scatter.2.cloned.1.call-start
  7.3 79.2 %all-gather.4.cloned.1.call-done = bf16[1024,4096]{1,0:T(8,128)(2,1)} async-done(((bf16[64,4096]{1,0:T(8,128)(2,1)}), bf16[1024,4096]{1,0:T(8,128)(2,1)}) %all-gather.4.cloned.1.call-update) | async-done | bytes 8388624 | tf_op jit(solution)/shard_map/all_gather | solution.py:28
  86.5 14.7 %convolution_convert_fusion = bf16[1024,1024]{1,0:T(8,128)(2,1)} fusion(bf16[1024,4096]{1,0:T(8,128)(2,1)} %param.3, bf16[1024,4096]{1,0:T(8,128)(2,1)} %all-gather.4.cloned.1.call-done), kind=kOutput, calls=%fused_computation.6 | convolution fusion | flops 8590983168 | bytes 18874368 | tf_op jit(solution)/shard_map/dot_general | solution.py:26
  101.3 0.0 reduce-scatter.2.cloned.1.call-update
  101.3 0.0 copy-start.1
  101.3 5.1 %multiply_reduce_fusion = f32[1024]{0:T(1024)S(1)} fusion(bf16[1024,4096]{1,0:T(8,128)(2,1)} %param.3), kind=kLoop, calls=%fused_computation | loop fusion | flops 12581888 | bytes 8392704 | tf_op jit(solution)/shard_map/reduce_sum | solution.py:24
  106.4 5.1 %psum.14 = f32[1024]{0:T(1024)S(1)} all-reduce(f32[1024]{0:T(1024)S(1)} %multiply_reduce_fusion), channel_id=1, replica_groups=mesh['rows'=16,'feat'=2] {'feat'}, use_global_device_ids=true, to_apply=%region_2.0 | all-reduce | flops 1024 | bytes 8192 | tf_op jit(solution)/shard_map/psum | solution.py:25
  111.5 0.0 copy-done.1
  111.6 20.5 %reduce-scatter.2.cloned.1.call-done = bf16[1024,512]{1,0:T(8,128)(2,1)} async-done(((bf16[1024,1024]{1,0:T(8,128)(2,1)}), bf16[1024,512]{1,0:T(8,128)(2,1)}) %reduce-scatter.2.cloned.1.call-update) | async-done | bytes 1048592 | tf_op jit(solution)/shard_map/reduce_scatter | solution.py:34
  132.1 0.0 copy-start
  132.1 1.6 fusion.1
  133.7 33.0 %psum.15 = f32[512]{0:T(512)S(1)} all-reduce(f32[512]{0:T(512)S(1)} %fusion.1), channel_id=1, replica_groups=mesh['rows'=16,'feat'=2] {'rows'}, use_global_device_ids=true, to_apply=%region_4.0 | all-reduce | flops 512 | bytes 4096 | tf_op jit(solution)/shard_map/psum | solution.py:39
  166.7 1.6 multiply_reduce_fusion.1
  168.3 17.2 %all-gather.1 = f32[16,1,512]{2,1,0:T(1,128)S(1)} all-gather(f32[1,1,512]{2,1,0:T(1,128)S(1)} %bitcast.3), channel_id=2, replica_groups=mesh['rows'=16,'feat'=2] {'rows'}, dimensions={0}, use_global_device_ids=true | all-gather | bytes 34816 | tf_op jit(solution)/shard_map/all_gather | solution.py:13
  185.6 0.0 copy-done
  185.6 1.3 multiply_convert_fusion
  (4 shorter events, 0.1 us)
Async XLA Ops:
  6.5 80.0 %all-gather.4.cloned.1.call-start = ((), (), s32[]{:S(2)}) async-start(), calls=%async_computation.1 | async-start | bytes 8912896 | tf_op jit(solution)/shard_map/all_gather | solution.py:28
  7.3 124.8 %reduce-scatter.2.cloned.1.call-start = ((), (), s32[]{:S(2)}) async-start(), calls=%async_computation.2 | async-start | bytes 3145728 | tf_op jit(solution)/shard_map/reduce_scatter | solution.py:34
  101.3 10.2 %copy-start.1 = (f32[1024]{0:T(1024)S(1)}, f32[1024]{0:T(1024)}, u32[]{:S(2)}) copy-start(f32[1024]{0:T(1024)} %param.5) | copy-start | bytes 12292
  132.1 53.6 %copy-start = (bf16[1024,512]{1,0:T(8,128)(2,1)S(1)}, bf16[1024,512]{1,0:T(8,128)(2,1)}, u32[]{:S(2)}) copy-start(bf16[1024,512]{1,0:T(8,128)(2,1)} %reduce-scatter.2.cloned.1.call-done) | copy-start | bytes 3145732
Sparse Core Ops, SparseCore 0:
  9.5 77.0 all-gather.3
  101.4 30.5 reduce-scatter.1
